TPU v7x, 32 devices: a whole 2x2x4 slice. The times are simulated.
32 devices in a mesh: tm: 8 (over z, x), space: 4 (over y, core).
Axes of the slice: x: 2, y: 2, z: 4, core: 2. Of those that a mesh axis runs over, the one named last changes fastest.
Arguments:
- forcing: float32 [8, 16, 32, 1024], P('tm', 'space'), may hold values from -6 to 6
- inv_density: bfloat16 [8, 16, 32, 1024], P('tm', 'space'), may hold values from 0.049804688 to 0.5
- wall_mask: int32 [16, 32, 1024], P('space'), may hold values 0 or 1
- guess: float32 [8, 16, 32, 1024], P('tm', 'space'), may hold values from -4 to 4
Outputs:
- pressure: float32 [8, 16, 32, 1024], P('tm', 'space')
- residual: float32 [8, 16, 32, 1024], P('tm', 'space')
All inputs are finite; a program needn't handle non-finite values. No bound on the sum of `wall_mask` on one device may be relied on, other than what follows from the above.
Results may differ from a plain program's by a relative error of at most 0.0003.
Values sent between devices are 32-bit elements; how exact they have to be, the bound alone decides.
A program may use at most 64 MiB of HBM per device.

v0:
```python
import jax
import jax.numpy as jnp
from jax import lax
from jax.sharding import PartitionSpec as P

SWEEPS = 2
ITERS = 2


def padded_2(cells, sides, width):
    for axis, dim in sides:
        count = lax.axis_size(axis)
        ends = count - 1
        head = lax.slice_in_dim(cells, 0, width, axis=dim)
        tail = lax.slice_in_dim(cells, cells.shape[dim] - width, cells.shape[dim], axis=dim)
        cells = jnp.concatenate(
            [
                lax.ppermute(tail, axis, [(i, (i + 1) % count) for i in range(ends)]),
                cells,
                lax.ppermute(head, axis, [((i + 1) % count, i) for i in range(ends)]),
            ],
            axis=dim,
        )
    return cells


def from_behind(block, axis, distance):
    devices = range(lax.axis_size(axis))
    route = [((i - distance) % len(devices), i) for i in devices]
    return lax.ppermute(block, axis, route)


def beside_all(extended):
    inner = extended[..., 1:-1, :, :]
    lead = [(0, 0)] * (inner.ndim - 2)
    padded = jnp.pad(inner, lead + [(1, 1), (1, 1)])
    beside = extended[..., 2:, :, :] + extended[..., :-2, :, :]
    beside = beside + padded[..., 2:, 1:-1] + padded[..., :-2, 1:-1]
    beside = beside + padded[..., 1:-1, 2:] + padded[..., 1:-1, :-2]
    return beside


def body(forcing, inv_density, wall_mask, guess):
    density_all = inv_density.astype(jnp.float32)
    mask_all = wall_mask.astype(jnp.float32)
    pressure = guess

    def extend_slab(field):
        return padded_2(field, (("space", 1),), 1)

    def earlier(field):
        return from_behind(field, "tm", 1)

    def two_earlier(field):
        return from_behind(field, "tm", 2)

    scale_down = 1.5 + 6.0 * density_all
    for it in range(ITERS):
        last_state = earlier(pressure)
        older_state = two_earlier(pressure)
        source = forcing + 2.0 * last_state - 0.5 * older_state
        value = pressure
        for sweep in range(SWEEPS):
            value = mask_all * (
                (source + density_all * beside_all(extend_slab(value))) / scale_down
            )
        pressure = value
    last_all = earlier(pressure)
    older_all = two_earlier(pressure)
    beside = beside_all(extend_slab(pressure))
    residual = mask_all * (
        forcing
        - 1.5 * pressure
        + 2.0 * last_all
        - 0.5 * older_all
        - density_all * (6.0 * pressure - beside)
    )
    return (pressure, residual)


def solution(mesh):
    placed = (
        P("tm", "space", None, None),
        P("tm", "space", None, None),
        P("space", None, None),
        P("tm", "space", None, None),
    )
    return jax.shard_map(
        body,
        mesh=mesh,
        in_specs=placed,
        out_specs=(P("tm", "space", None, None), P("tm", "space", None, None)),
        check_vma=False,
    )
```

profile of v0, /device:TPU:1, one launch (start us, length us, event | category | flops | bytes accessed | tf_op | source)
XLA Modules:
  0.0 96.1 jit_solution(23929177476151246)
XLA Ops:
  0.6 2.2 %collective-permute-start.1 = (f32[1,4,32,1024]{3,2,1,0:T(8,128)}, f32[1,4,32,1024]{3,2,1,0:T(8,128)S(1)}, u32[]{:S(2)}, u32[]{:S(2)}) collective-permute-start(f32[1,4,32,1024]{3,2,1,0:T(8,128)} %param.7), channel_id=1, source_target_pairs={{24,0},{28,4},{0,8},{4,12},{8,16},{12,20},{16,24},{20,28},{25,1},{... | collective-permute-start | bytes 1572872 | tf_op jit(solution)/shard_map/ppermute | solution.py:30
  2.8 1.2 %collective-permute-start = (f32[1,4,32,1024]{3,2,1,0:T(8,128)}, f32[1,4,32,1024]{3,2,1,0:T(8,128)S(1)}, u32[]{:S(2)}, u32[]{:S(2)}) collective-permute-start(f32[1,4,32,1024]{3,2,1,0:T(8,128)} %param.7), channel_id=1, source_target_pairs={{28,0},{0,4},{4,8},{8,12},{12,16},{16,20},{20,24},{24,28},{29,1},{... | collective-permute-start | bytes 1572872 | tf_op jit(solution)/shard_map/ppermute | solution.py:30
  5.0 3.1 %collective-permute-start.2 = (f32[1,1,32,1024]{3,2,1,0:T(8,128)S(1)}, f32[1,1,32,1024]{3,2,1,0:T(8,128)S(1)}, u32[]{:S(2)}, u32[]{:S(2)}) collective-permute-start(f32[1,1,32,1024]{3,2,1,0:T(8,128)S(1)} %get-tuple-element.10), channel_id=1, source_target_pairs={{1,0},{2,1},{3,2},{5,4},{6,5},{7,6},{9,8},{10,9},{11,10},{13,12},{... | collective-permute-start | bytes 393224 | tf_op jit(solution)/shard_map/ppermute | solution.py:20
  8.2 3.0 %collective-permute-start.3 = (f32[1,1,32,1024]{3,2,1,0:T(8,128)S(1)}, f32[1,1,32,1024]{3,2,1,0:T(8,128)S(1)}, u32[]{:S(2)}, u32[]{:S(2)}) collective-permute-start(f32[1,1,32,1024]{3,2,1,0:T(8,128)S(1)} %get-tuple-element.11), channel_id=1, source_target_pairs={{0,1},{1,2},{2,3},{4,5},{5,6},{6,7},{8,9},{9,10},{10,11},{12,13},{... | collective-permute-start | bytes 393224 | tf_op jit(solution)/shard_map/ppermute | solution.py:18
  13.1 3.5 %collective-permute-done.1 = f32[1,4,32,1024]{3,2,1,0:T(8,128)S(1)} collective-permute-done((f32[1,4,32,1024]{3,2,1,0:T(8,128)}, f32[1,4,32,1024]{3,2,1,0:T(8,128)S(1)}, u32[]{:S(2)}, u32[]{:S(2)}) %collective-permute-start.1) | collective-permute-done | bytes 524320 | tf_op jit(solution)/shard_map/ppermute | solution.py:30
  16.7 11.9 %collective-permute-done = f32[1,4,32,1024]{3,2,1,0:T(8,128)S(1)} collective-permute-done((f32[1,4,32,1024]{3,2,1,0:T(8,128)}, f32[1,4,32,1024]{3,2,1,0:T(8,128)S(1)}, u32[]{:S(2)}, u32[]{:S(2)}) %collective-permute-start) | collective-permute-done | bytes 524320 | tf_op jit(solution)/shard_map/ppermute | solution.py:30
  28.6 2.9 %bitcast_multiply_fusion = f32[1,4,32,1024]{3,2,1,0:T(8,128)S(1)} fusion(s32[4,32,1024]{2,1,0:T(8,128)S(1)} %copy-done, f32[1,4,32,1024]{3,2,1,0:T(8,128)} %param.7, f32[1,1,32,1024]{3,2,1,0:T(8,128)S(1)} %collective-permute-done.3, f32[1,1,32,1024]{3,2,1,0:T(8,128)S(1)} %collective-permute-done.2, bf16[1,4,32,1024]{3,2,1,0:T(8,128)(2,1)} %param.5, ...), kind=kLoop, calls=%fused_computation.76 | loop fusion | flops 2490368 | bytes 3670016 | tf_op jit(solution)/shard_map/mul | solution.py:64
  31.6 3.5 %collective-permute-start.4 = (f32[1,1,32,1024]{3,2,1,0:T(8,128)S(1)}, f32[1,1,32,1024]{3,2,1,0:T(8,128)S(1)}, u32[]{:S(2)}, u32[]{:S(2)}) collective-permute-start(f32[1,1,32,1024]{3,2,1,0:T(8,128)S(1)} %get-tuple-element.8), channel_id=1, source_target_pairs={{1,0},{2,1},{3,2},{5,4},{6,5},{7,6},{9,8},{10,9},{11,10},{13,12},{... | collective-permute-start | bytes 393224 | tf_op jit(solution)/shard_map/ppermute | solution.py:20
  35.1 3.0 %collective-permute-start.5 = (f32[1,1,32,1024]{3,2,1,0:T(8,128)S(1)}, f32[1,1,32,1024]{3,2,1,0:T(8,128)S(1)}, u32[]{:S(2)}, u32[]{:S(2)}) collective-permute-start(f32[1,1,32,1024]{3,2,1,0:T(8,128)S(1)} %get-tuple-element.9), channel_id=1, source_target_pairs={{0,1},{1,2},{2,3},{4,5},{5,6},{6,7},{8,9},{9,10},{10,11},{12,13},{... | collective-permute-start | bytes 393224 | tf_op jit(solution)/shard_map/ppermute | solution.py:18
  38.8 1.2 %collective-permute-done.5 = f32[1,1,32,1024]{3,2,1,0:T(8,128)S(1)} collective-permute-done((f32[1,1,32,1024]{3,2,1,0:T(8,128)S(1)}, f32[1,1,32,1024]{3,2,1,0:T(8,128)S(1)}, u32[]{:S(2)}, u32[]{:S(2)}) %collective-permute-start.5) | collective-permute-done | bytes 131104 | tf_op jit(solution)/shard_map/ppermute | solution.py:18
  40.8 1.9 %collective-permute-start.8 = (f32[1,1,32,1024]{3,2,1,0:T(8,128)S(1)}, f32[1,1,32,1024]{3,2,1,0:T(8,128)S(1)}, u32[]{:S(2)}, u32[]{:S(2)}) collective-permute-start(f32[1,1,32,1024]{3,2,1,0:T(8,128)S(1)} %get-tuple-element.6), channel_id=1, source_target_pairs={{1,0},{2,1},{3,2},{5,4},{6,5},{7,6},{9,8},{10,9},{11,10},{13,12},{... | collective-permute-start | bytes 393224 | tf_op jit(solution)/shard_map/ppermute | solution.py:20
  42.7 4.4 %collective-permute-start.9 = (f32[1,1,32,1024]{3,2,1,0:T(8,128)S(1)}, f32[1,1,32,1024]{3,2,1,0:T(8,128)S(1)}, u32[]{:S(2)}, u32[]{:S(2)}) collective-permute-start(f32[1,1,32,1024]{3,2,1,0:T(8,128)S(1)} %get-tuple-element.7), channel_id=1, source_target_pairs={{0,1},{1,2},{2,3},{4,5},{5,6},{6,7},{8,9},{9,10},{10,11},{12,13},{... | collective-permute-start | bytes 393224 | tf_op jit(solution)/shard_map/ppermute | solution.py:18
  47.1 1.0 %collective-permute-done.8 = f32[1,1,32,1024]{3,2,1,0:T(8,128)S(1)} collective-permute-done((f32[1,1,32,1024]{3,2,1,0:T(8,128)S(1)}, f32[1,1,32,1024]{3,2,1,0:T(8,128)S(1)}, u32[]{:S(2)}, u32[]{:S(2)}) %collective-permute-start.8) | collective-permute-done | bytes 131104 | tf_op jit(solution)/shard_map/ppermute | solution.py:20
  49.0 6.3 %collective-permute-done.7 = f32[1,4,32,1024]{3,2,1,0:T(8,128)S(1)} collective-permute-done((f32[1,4,32,1024]{3,2,1,0:T(8,128)S(1)}, f32[1,4,32,1024]{3,2,1,0:T(8,128)S(1)}, u32[]{:S(2)}, u32[]{:S(2)}) %collective-permute-start.7) | collective-permute-done | bytes 524320 | tf_op jit(solution)/shard_map/ppermute | solution.py:30
  55.3 8.3 %collective-permute-done.6 = f32[1,4,32,1024]{3,2,1,0:T(8,128)S(1)} collective-permute-done((f32[1,4,32,1024]{3,2,1,0:T(8,128)S(1)}, f32[1,4,32,1024]{3,2,1,0:T(8,128)S(1)}, u32[]{:S(2)}, u32[]{:S(2)}) %collective-permute-start.6) | collective-permute-done | bytes 524320 | tf_op jit(solution)/shard_map/ppermute | solution.py:30
  64.1 1.9 %collective-permute-start.10 = (f32[1,1,32,1024]{3,2,1,0:T(8,128)S(1)}, f32[1,1,32,1024]{3,2,1,0:T(8,128)S(1)}, u32[]{:S(2)}, u32[]{:S(2)}) collective-permute-start(f32[1,1,32,1024]{3,2,1,0:T(8,128)S(1)} %get-tuple-element.4), channel_id=1, source_target_pairs={{1,0},{2,1},{3,2},{5,4},{6,5},{7,6},{9,8},{10,9},{11,10},{13,12},{... | collective-permute-start | bytes 393224 | tf_op jit(solution)/shard_map/ppermute | solution.py:20
  66.1 3.6 %collective-permute-start.11 = (f32[1,1,32,1024]{3,2,1,0:T(8,128)S(1)}, f32[1,1,32,1024]{3,2,1,0:T(8,128)S(1)}, u32[]{:S(2)}, u32[]{:S(2)}) collective-permute-start(f32[1,1,32,1024]{3,2,1,0:T(8,128)S(1)} %get-tuple-element.5), channel_id=1, source_target_pairs={{0,1},{1,2},{2,3},{4,5},{5,6},{6,7},{8,9},{9,10},{10,11},{12,13},{... | collective-permute-start | bytes 393224 | tf_op jit(solution)/shard_map/ppermute | solution.py:18
  70.4 1.2 %collective-permute-done.11 = f32[1,1,32,1024]{3,2,1,0:T(8,128)S(1)} collective-permute-done((f32[1,1,32,1024]{3,2,1,0:T(8,128)S(1)}, f32[1,1,32,1024]{3,2,1,0:T(8,128)S(1)}, u32[]{:S(2)}, u32[]{:S(2)}) %collective-permute-start.11) | collective-permute-done | bytes 131104 | tf_op jit(solution)/shard_map/ppermute | solution.py:18
  72.4 1.9 %collective-permute-start.14 = (f32[1,1,32,1024]{3,2,1,0:T(8,128)S(1)}, f32[1,1,32,1024]{3,2,1,0:T(8,128)S(1)}, u32[]{:S(2)}, u32[]{:S(2)}) collective-permute-start(f32[1,1,32,1024]{3,2,1,0:T(8,128)S(1)} %get-tuple-element.2), channel_id=1, source_target_pairs={{1,0},{2,1},{3,2},{5,4},{6,5},{7,6},{9,8},{10,9},{11,10},{13,12},{... | collective-permute-start | bytes 393224 | tf_op jit(solution)/shard_map/ppermute | solution.py:20
  74.3 4.4 %collective-permute-start.15 = (f32[1,1,32,1024]{3,2,1,0:T(8,128)S(1)}, f32[1,1,32,1024]{3,2,1,0:T(8,128)S(1)}, u32[]{:S(2)}, u32[]{:S(2)}) collective-permute-start(f32[1,1,32,1024]{3,2,1,0:T(8,128)S(1)} %get-tuple-element.3), channel_id=1, source_target_pairs={{0,1},{1,2},{2,3},{4,5},{5,6},{6,7},{8,9},{9,10},{10,11},{12,13},{... | collective-permute-start | bytes 393224 | tf_op jit(solution)/shard_map/ppermute | solution.py:18
  78.6 1.0 %collective-permute-done.14 = f32[1,1,32,1024]{3,2,1,0:T(8,128)S(1)} collective-permute-done((f32[1,1,32,1024]{3,2,1,0:T(8,128)S(1)}, f32[1,1,32,1024]{3,2,1,0:T(8,128)S(1)}, u32[]{:S(2)}, u32[]{:S(2)}) %collective-permute-start.14) | collective-permute-done | bytes 131104 | tf_op jit(solution)/shard_map/ppermute | solution.py:20
  80.6 5.7 %collective-permute-done.13 = f32[1,4,32,1024]{3,2,1,0:T(8,128)S(1)} collective-permute-done((f32[1,4,32,1024]{3,2,1,0:T(8,128)S(1)}, f32[1,4,32,1024]{3,2,1,0:T(8,128)S(1)}, u32[]{:S(2)}, u32[]{:S(2)}) %collective-permute-start.13) | collective-permute-done | bytes 524320 | tf_op jit(solution)/shard_map/ppermute | solution.py:30
  86.3 8.5 %collective-permute-done.12 = f32[1,4,32,1024]{3,2,1,0:T(8,128)S(1)} collective-permute-done((f32[1,4,32,1024]{3,2,1,0:T(8,128)S(1)}, f32[1,4,32,1024]{3,2,1,0:T(8,128)S(1)}, u32[]{:S(2)}, u32[]{:S(2)}) %collective-permute-start.12) | collective-permute-done | bytes 524320 | tf_op jit(solution)/shard_map/ppermute | solution.py:30
  94.8 1.3 %fusion.34 = f32[1,4,32,1024]{3,2,1,0:T(8,128)} fusion(f32[1,4,32,1024]{3,2,1,0:T(8,128)S(1)} %fusion.29, bf16[1,4,32,1024]{3,2,1,0:T(8,128)(2,1)S(1)} %copy-done.2, f32[1,1,32,1024]{3,2,1,0:T(8,128)S(1)} %collective-permute-done.15, f32[1,1,32,1024]{3,2,1,0:T(8,128)S(1)} %collective-permute-done.14, f32[1,4,32,1024]{3,2,1,0:T(8,128)S(1)} %collective-permute-done.13, ...), kind=kLoop, calls=%fused_computation.60 | loop fusion | flops 2621440 | bytes 3670016 | tf_op jit(solution)/shard_map/mul | solution.py:71
  (26 shorter events, 8.1 us)
Async XLA Ops:
  0.6 28.0 %copy-start = (s32[4,32,1024]{2,1,0:T(8,128)S(1)}, s32[4,32,1024]{2,1,0:T(8,128)}, u32[]{:S(2)}) copy-start(s32[4,32,1024]{2,1,0:T(8,128)} %param.6) | copy-start | bytes 1572868
  0.6 16.0 %collective-permute-start.1 = (f32[1,4,32,1024]{3,2,1,0:T(8,128)}, f32[1,4,32,1024]{3,2,1,0:T(8,128)S(1)}, u32[]{:S(2)}, u32[]{:S(2)}) collective-permute-start(f32[1,4,32,1024]{3,2,1,0:T(8,128)} %param.7), channel_id=1, source_target_pairs={{24,0},{28,4},{0,8},{4,12},{8,16},{12,20},{16,24},{20,28},{25,1},{... | collective-permute-start | bytes 1572872 | tf_op jit(solution)/shard_map/ppermute | solution.py:30
  2.8 25.8 %collective-permute-start = (f32[1,4,32,1024]{3,2,1,0:T(8,128)}, f32[1,4,32,1024]{3,2,1,0:T(8,128)S(1)}, u32[]{:S(2)}, u32[]{:S(2)}) collective-permute-start(f32[1,4,32,1024]{3,2,1,0:T(8,128)} %param.7), channel_id=1, source_target_pairs={{28,0},{0,4},{4,8},{8,12},{12,16},{16,20},{20,24},{24,28},{29,1},{... | collective-permute-start | bytes 1572872 | tf_op jit(solution)/shard_map/ppermute | solution.py:30
  5.0 7.2 %collective-permute-start.2 = (f32[1,1,32,1024]{3,2,1,0:T(8,128)S(1)}, f32[1,1,32,1024]{3,2,1,0:T(8,128)S(1)}, u32[]{:S(2)}, u32[]{:S(2)}) collective-permute-start(f32[1,1,32,1024]{3,2,1,0:T(8,128)S(1)} %get-tuple-element.10), channel_id=1, source_target_pairs={{1,0},{2,1},{3,2},{5,4},{6,5},{7,6},{9,8},{10,9},{11,10},{13,12},{... | collective-permute-start | bytes 393224 | tf_op jit(solution)/shard_map/ppermute | solution.py:20
  8.2 5.0 %collective-permute-start.3 = (f32[1,1,32,1024]{3,2,1,0:T(8,128)S(1)}, f32[1,1,32,1024]{3,2,1,0:T(8,128)S(1)}, u32[]{:S(2)}, u32[]{:S(2)}) collective-permute-start(f32[1,1,32,1024]{3,2,1,0:T(8,128)S(1)} %get-tuple-element.11), channel_id=1, source_target_pairs={{0,1},{1,2},{2,3},{4,5},{5,6},{6,7},{8,9},{9,10},{10,11},{12,13},{... | collective-permute-start | bytes 393224 | tf_op jit(solution)/shard_map/ppermute | solution.py:18
  28.6 11.4 %copy-start.2 = (bf16[1,4,32,1024]{3,2,1,0:T(8,128)(2,1)S(1)}, bf16[1,4,32,1024]{3,2,1,0:T(8,128)(2,1)}, u32[]{:S(2)}) copy-start(bf16[1,4,32,1024]{3,2,1,0:T(8,128)(2,1)} %param.5) | copy-start | bytes 786436
  31.5 8.5 %copy-start.1 = (f32[1,4,32,1024]{3,2,1,0:T(8,128)S(1)}, f32[1,4,32,1024]{3,2,1,0:T(8,128)}, u32[]{:S(2)}) copy-start(f32[1,4,32,1024]{3,2,1,0:T(8,128)} %param.4) | copy-start | bytes 1572868
  31.6 7.3 %collective-permute-start.4 = (f32[1,1,32,1024]{3,2,1,0:T(8,128)S(1)}, f32[1,1,32,1024]{3,2,1,0:T(8,128)S(1)}, u32[]{:S(2)}, u32[]{:S(2)}) collective-permute-start(f32[1,1,32,1024]{3,2,1,0:T(8,128)S(1)} %get-tuple-element.8), channel_id=1, source_target_pairs={{1,0},{2,1},{3,2},{5,4},{6,5},{7,6},{9,8},{10,9},{11,10},{13,12},{... | collective-permute-start | bytes 393224 | tf_op jit(solution)/shard_map/ppermute | solution.py:20
  35.1 5.0 %collective-permute-start.5 = (f32[1,1,32,1024]{3,2,1,0:T(8,128)S(1)}, f32[1,1,32,1024]{3,2,1,0:T(8,128)S(1)}, u32[]{:S(2)}, u32[]{:S(2)}) collective-permute-start(f32[1,1,32,1024]{3,2,1,0:T(8,128)S(1)} %get-tuple-element.9), channel_id=1, source_target_pairs={{0,1},{1,2},{2,3},{4,5},{5,6},{6,7},{8,9},{9,10},{10,11},{12,13},{... | collective-permute-start | bytes 393224 | tf_op jit(solution)/shard_map/ppermute | solution.py:18
  40.6 14.7 %collective-permute-start.7 = (f32[1,4,32,1024]{3,2,1,0:T(8,128)S(1)}, f32[1,4,32,1024]{3,2,1,0:T(8,128)S(1)}, u32[]{:S(2)}, u32[]{:S(2)}) collective-permute-start(f32[1,4,32,1024]{3,2,1,0:T(8,128)S(1)} %fusion.27), channel_id=1, source_target_pairs={{24,0},{28,4},{0,8},{4,12},{8,16},{12,20},{16,24},{20,28},{25,1},{... | collective-permute-start | bytes 1572872 | tf_op jit(solution)/shard_map/ppermute | solution.py:30
  40.7 22.9 %collective-permute-start.6 = (f32[1,4,32,1024]{3,2,1,0:T(8,128)S(1)}, f32[1,4,32,1024]{3,2,1,0:T(8,128)S(1)}, u32[]{:S(2)}, u32[]{:S(2)}) collective-permute-start(f32[1,4,32,1024]{3,2,1,0:T(8,128)S(1)} %fusion.27), channel_id=1, source_target_pairs={{28,0},{0,4},{4,8},{8,12},{12,16},{16,20},{20,24},{24,28},{29,1},{... | collective-permute-start | bytes 1572872 | tf_op jit(solution)/shard_map/ppermute | solution.py:30
  40.8 7.3 %collective-permute-start.8 = (f32[1,1,32,1024]{3,2,1,0:T(8,128)S(1)}, f32[1,1,32,1024]{3,2,1,0:T(8,128)S(1)}, u32[]{:S(2)}, u32[]{:S(2)}) collective-permute-start(f32[1,1,32,1024]{3,2,1,0:T(8,128)S(1)} %get-tuple-element.6), channel_id=1, source_target_pairs={{1,0},{2,1},{3,2},{5,4},{6,5},{7,6},{9,8},{10,9},{11,10},{13,12},{... | collective-permute-start | bytes 393224 | tf_op jit(solution)/shard_map/ppermute | solution.py:20
  42.7 6.3 %collective-permute-start.9 = (f32[1,1,32,1024]{3,2,1,0:T(8,128)S(1)}, f32[1,1,32,1024]{3,2,1,0:T(8,128)S(1)}, u32[]{:S(2)}, u32[]{:S(2)}) collective-permute-start(f32[1,1,32,1024]{3,2,1,0:T(8,128)S(1)} %get-tuple-element.7), channel_id=1, source_target_pairs={{0,1},{1,2},{2,3},{4,5},{5,6},{6,7},{8,9},{9,10},{10,11},{12,13},{... | collective-permute-start | bytes 393224 | tf_op jit(solution)/shard_map/ppermute | solution.py:18
  64.1 6.3 %collective-permute-start.10 = (f32[1,1,32,1024]{3,2,1,0:T(8,128)S(1)}, f32[1,1,32,1024]{3,2,1,0:T(8,128)S(1)}, u32[]{:S(2)}, u32[]{:S(2)}) collective-permute-start(f32[1,1,32,1024]{3,2,1,0:T(8,128)S(1)} %get-tuple-element.4), channel_id=1, source_target_pairs={{1,0},{2,1},{3,2},{5,4},{6,5},{7,6},{9,8},{10,9},{11,10},{13,12},{... | collective-permute-start | bytes 393224 | tf_op jit(solution)/shard_map/ppermute | solution.py:20
  66.1 5.6 %collective-permute-start.11 = (f32[1,1,32,1024]{3,2,1,0:T(8,128)S(1)}, f32[1,1,32,1024]{3,2,1,0:T(8,128)S(1)}, u32[]{:S(2)}, u32[]{:S(2)}) collective-permute-start(f32[1,1,32,1024]{3,2,1,0:T(8,128)S(1)} %get-tuple-element.5), channel_id=1, source_target_pairs={{0,1},{1,2},{2,3},{4,5},{5,6},{6,7},{8,9},{9,10},{10,11},{12,13},{... | collective-permute-start | bytes 393224 | tf_op jit(solution)/shard_map/ppermute | solution.py:18
  72.2 24.0 %copy-start.3 = (f32[1,4,32,1024]{3,2,1,0:T(8,128)}, f32[1,4,32,1024]{3,2,1,0:T(8,128)S(1)}, u32[]{:S(2)}) copy-start(f32[1,4,32,1024]{3,2,1,0:T(8,128)S(1)} %fusion.29) | copy-start | bytes 1572868
  72.2 14.1 %collective-permute-start.13 = (f32[1,4,32,1024]{3,2,1,0:T(8,128)S(1)}, f32[1,4,32,1024]{3,2,1,0:T(8,128)S(1)}, u32[]{:S(2)}, u32[]{:S(2)}) collective-permute-start(f32[1,4,32,1024]{3,2,1,0:T(8,128)S(1)} %fusion.29), channel_id=1, source_target_pairs={{24,0},{28,4},{0,8},{4,12},{8,16},{12,20},{16,24},{20,28},{25,1},{... | collective-permute-start | bytes 1572872 | tf_op jit(solution)/shard_map/ppermute | solution.py:30
  72.3 22.5 %collective-permute-start.12 = (f32[1,4,32,1024]{3,2,1,0:T(8,128)S(1)}, f32[1,4,32,1024]{3,2,1,0:T(8,128)S(1)}, u32[]{:S(2)}, u32[]{:S(2)}) collective-permute-start(f32[1,4,32,1024]{3,2,1,0:T(8,128)S(1)} %fusion.29), channel_id=1, source_target_pairs={{28,0},{0,4},{4,8},{8,12},{12,16},{16,20},{20,24},{24,28},{29,1},{... | collective-permute-start | bytes 1572872 | tf_op jit(solution)/shard_map/ppermute | solution.py:30
  72.4 7.3 %collective-permute-start.14 = (f32[1,1,32,1024]{3,2,1,0:T(8,128)S(1)}, f32[1,1,32,1024]{3,2,1,0:T(8,128)S(1)}, u32[]{:S(2)}, u32[]{:S(2)}) collective-permute-start(f32[1,1,32,1024]{3,2,1,0:T(8,128)S(1)} %get-tuple-element.2), channel_id=1, source_target_pairs={{1,0},{2,1},{3,2},{5,4},{6,5},{7,6},{9,8},{10,9},{11,10},{13,12},{... | collective-permute-start | bytes 393224 | tf_op jit(solution)/shard_map/ppermute | solution.py:20
  74.3 6.3 %collective-permute-start.15 = (f32[1,1,32,1024]{3,2,1,0:T(8,128)S(1)}, f32[1,1,32,1024]{3,2,1,0:T(8,128)S(1)}, u32[]{:S(2)}, u32[]{:S(2)}) collective-permute-start(f32[1,1,32,1024]{3,2,1,0:T(8,128)S(1)} %get-tuple-element.3), channel_id=1, source_target_pairs={{0,1},{1,2},{2,3},{4,5},{5,6},{6,7},{8,9},{9,10},{10,11},{12,13},{... | collective-permute-start | bytes 393224 | tf_op jit(solution)/shard_map/ppermute | solution.py:18
where the time goes:
time: 96.5 us; the launch traced here: 96.1 us
  waiting for transfers between devices  53.9 us (56%)
  starting transfers between devices  34.5 us (36%)
  other arithmetic  5.88 us (6%)
  local copies, waits for them, and re-layouts  1.09 us (1%)
    ppermute x6, waiting for transfers between devices, from_behind(): return lax.ppermute(block, axis, route)  44.3 us
    ppermute x5, starting transfers between devices, padded_2(): lax.ppermute(tail, axis, [(i, (i + 1) % count) for i in range(ends)])  18.4 us
    ppermute x5, starting transfers between devices, padded_2(): lax.ppermute(head, axis, [((i + 1) % count, i) for i in range(ends)])  12.4 us
    ppermute x5, waiting for transfers between devices, padded_2(): lax.ppermute(tail, axis, [(i, (i + 1) % count) for i in range(ends)])  5.2 us
    mul x4, other arithmetic, body(): mask_all * ((source + density_all * beside_all(extend_slab(value))) / sca...  4.54 us
    ppermute x5, waiting for transfers between devices, padded_2(): lax.ppermute(head, axis, [((i + 1) % count, i) for i in range(ends)])  4.43 us
    ppermute x6, starting transfers between devices, from_behind(): return lax.ppermute(block, axis, route)  3.61 us
  transfers between devices with their start and end apart: 16, of which 16 were waited for; matrix products, arithmetic and copies ran while one was open for 1% of the time, Pallas kernels for 0%

commit v1 on v0

v1 whole, which is shorter than its diff:
```python
import functools

import jax
import jax.numpy as jnp
from jax import lax
from jax.experimental import pallas as pl
from jax.experimental.pallas import tpu as pltpu
from jax.sharding import PartitionSpec as P

ITERS = 2
ROWS = 8
PAD = 8


def kernel(
    n_tm, n_space,
    f_hbm, k_hbm, m_hbm, g_hbm, p_out, r_out,
    V, A, B, F, K, M, W, KW, MD, MK, G, R,
    load_sem, out_sem, sa, ra, sb, rb, sh, rh,
):
    planes, height, width = F.shape
    chunks = height // ROWS
    t = lax.axis_index("tm")
    s = lax.axis_index("space")
    even = lax.rem(t, 2) == 0
    odd = lax.rem(t, 2) == 1
    partner = t + 1 - 2 * lax.rem(t, 2)
    ahead = lax.rem(t + 2, n_tm)
    behind = lax.rem(t + n_tm - 2, n_tm)
    has_lo = s > 0
    has_hi = s < n_space - 1

    def rows(c):
        return pl.ds(c * ROWS, ROWS)

    def padded(c):
        return pl.ds(PAD + c * ROWS, ROWS)

    loads = [
        pltpu.make_async_copy(g_hbm.at[0], V.at[0, pl.ds(1, planes), pl.ds(PAD, height)], load_sem.at[0]),
        pltpu.make_async_copy(k_hbm.at[0], K, load_sem.at[1]),
        pltpu.make_async_copy(m_hbm, M, load_sem.at[2]),
        pltpu.make_async_copy(f_hbm.at[0], F, load_sem.at[3]),
    ]
    for load in loads:
        load.start()

    barrier = pltpu.get_barrier_semaphore()
    for other in (partner, ahead, behind):
        pl.semaphore_signal(barrier, inc=1, device_id={"tm": other}, device_id_type=pl.DeviceIdType.MESH)

    @pl.when(has_lo)
    def _():
        pl.semaphore_signal(barrier, inc=1, device_id={"space": s - 1}, device_id_type=pl.DeviceIdType.MESH)

    @pl.when(has_hi)
    def _():
        pl.semaphore_signal(barrier, inc=1, device_id={"space": s + 1}, device_id_type=pl.DeviceIdType.MESH)

    @pl.when(has_lo & has_hi)
    def _():
        pl.semaphore_wait(barrier, 5)

    @pl.when(jnp.logical_not(has_lo & has_hi))
    def _():
        pl.semaphore_wait(barrier, 4)

    def field(e, c):
        if e == 0:
            return g_hbm.at[0, :, rows(c)]
        return V.at[2 * e, pl.ds(1, planes), padded(c)]

    def to_ahead(e, c):
        return pltpu.make_async_remote_copy(
            field(e, c), B.at[e, :, rows(c)], sb.at[e, c], rb.at[e, c],
            device_id={"tm": ahead}, device_id_type=pl.DeviceIdType.MESH)

    def to_partner(e, c):
        return pltpu.make_async_remote_copy(
            field(e, c), A.at[e, :, rows(c)], sa.at[e, c], ra.at[e, c],
            device_id={"tm": partner}, device_id_type=pl.DeviceIdType.MESH)

    def relay(e, c):
        return pltpu.make_async_remote_copy(
            B.at[e, :, rows(c)], A.at[e, :, rows(c)], sa.at[e, c], ra.at[e, c],
            device_id={"tm": partner}, device_id_type=pl.DeviceIdType.MESH)

    def to_lo(i, c):
        src = g_hbm.at[0, 0, rows(c)] if i == 0 else V.at[i, 1, padded(c)]
        return pltpu.make_async_remote_copy(
            src, V.at[i, planes + 1, padded(c)], sh.at[i, 0, c], rh.at[i, 1, c],
            device_id={"space": s - 1}, device_id_type=pl.DeviceIdType.MESH)

    def to_hi(i, c):
        src = g_hbm.at[0, planes - 1, rows(c)] if i == 0 else V.at[i, planes, padded(c)]
        return pltpu.make_async_remote_copy(
            src, V.at[i, 0, padded(c)], sh.at[i, 1, c], rh.at[i, 0, c],
            device_id={"space": s + 1}, device_id_type=pl.DeviceIdType.MESH)

    def send_field(e, c):
        to_ahead(e, c).start()

        @pl.when(even)
        def _():
            to_partner(e, c).start()

    def send_halo(i, c):
        @pl.when(has_lo)
        def _():
            to_lo(i, c).start()

        @pl.when(has_hi)
        def _():
            to_hi(i, c).start()

    def wait_halo(i, c):
        @pl.when(has_lo)
        def _():
            to_hi(i, c).wait_recv()

        @pl.when(has_hi)
        def _():
            to_lo(i, c).wait_recv()

    for c in range(chunks):
        send_field(0, c)
        send_halo(0, c)

    last = 2 * ITERS
    edge = jnp.zeros((PAD, width), jnp.float32)
    for i in range(last + 1):
        def clear(p, _, i=i):
            V[i, p, pl.ds(0, PAD), :] = edge
            V[i, p, pl.ds(PAD + height, PAD), :] = edge
            return 0
        lax.fori_loop(1, planes + 1, clear, 0)

        @pl.when(s == 0)
        def _(i=i):
            V[i, 0, pl.ds(PAD, height), :] = jnp.zeros((height, width), jnp.float32)

        @pl.when(s == n_space - 1)
        def _(i=i):
            V[i, planes + 1, pl.ds(PAD, height), :] = jnp.zeros((height, width), jnp.float32)

    for load in loads:
        load.wait()

    def prepare(p, _):
        for h in range(height // 16):
            at = pl.ds(16 * h, 16)
            k = K[p, at, :].astype(jnp.float32)
            m = M[p, at, :].astype(jnp.float32)
            d = 1.5 + 6.0 * k
            w = m / d
            W[p, at, :] = w
            KW[p, at, :] = k * w
            MD[p, at, :] = m * d
            MK[p, at, :] = m * k
        return 0

    lax.fori_loop(0, planes, prepare, 0)

    lane = lax.broadcasted_iota(jnp.int32, (ROWS, width), 1)

    def beside(i, p, c):
        mid = V[i, p + 1, padded(c), :]
        total = V[i, p, padded(c), :] + V[i, p + 2, padded(c), :]
        total = total + V[i, p + 1, pl.ds(PAD + c * ROWS - 1, ROWS), :]
        total = total + V[i, p + 1, pl.ds(PAD + c * ROWS + 1, ROWS), :]
        total = total + jnp.where(lane == 0, 0.0, pltpu.roll(mid, 1, 1))
        total = total + jnp.where(lane == width - 1, 0.0, pltpu.roll(mid, width - 1, 1))
        return mid, total

    def sweep_first(e, c):
        def step(p, _):
            at = rows(c)
            src = F[p, at, :] + 2.0 * A[e, p, at, :] - 0.5 * B[e, p, at, :]
            g = W[p, at, :] * src
            G[p, at, :] = g
            V[2 * e + 1, p + 1, padded(c), :] = g + KW[p, at, :] * beside(2 * e, p, c)[1]
            return 0
        lax.fori_loop(0, planes, step, 0)

    def sweep_second(e, c):
        def step(p, _):
            at = rows(c)
            V[2 * e + 2, p + 1, padded(c), :] = G[p, at, :] + KW[p, at, :] * beside(2 * e + 1, p, c)[1]
            return 0
        lax.fori_loop(0, planes, step, 0)

    def arrive(e, c):
        to_ahead(e, c).wait_recv()

        @pl.when(odd)
        def _():
            relay(e, c).start()

    def finish(e, c):
        wait_halo(2 * e + 1, c)
        sweep_second(e, c)
        send_field(e + 1, c)
        send_halo(2 * e + 2, c)
        if e == ITERS - 1:
            pltpu.make_async_copy(
                V.at[last, pl.ds(1, planes), padded(c)], p_out.at[0, :, rows(c)], out_sem.at[0, c]
            ).start()

    for e in range(ITERS):
        for c in range(chunks):
            arrive(e, c)
            wait_halo(2 * e, c)
            to_partner(e, c).wait_recv()
            sweep_first(e, c)
            send_halo(2 * e + 1, c)
            if c >= 1:
                finish(e, c - 1)
        finish(e, chunks - 1)

    for c in range(chunks):
        arrive(ITERS, c)
        wait_halo(last, c)

        def partial(p, _, c=c):
            at = rows(c)
            mid, total = beside(last, p, c)
            m = M[p, at, :].astype(jnp.float32)
            R[p, at, :] = m * F[p, at, :] - MD[p, at, :] * mid + MK[p, at, :] * total
            return 0
        lax.fori_loop(0, planes, partial, 0)
        to_partner(ITERS, c).wait_recv()

        def complete(p, _, c=c):
            at = rows(c)
            m = M[p, at, :].astype(jnp.float32)
            R[p, at, :] = R[p, at, :] + m * (2.0 * A[ITERS, p, at, :] - 0.5 * B[ITERS, p, at, :])
            return 0
        lax.fori_loop(0, planes, complete, 0)
        pltpu.make_async_copy(R.at[:, rows(c)], r_out.at[0, :, rows(c)], out_sem.at[1, c]).start()

    for e in range(ITERS + 1):
        for c in range(chunks):
            to_ahead(e, c).wait_send()

            @pl.when(even)
            def _(e=e, c=c):
                to_partner(e, c).wait_send()

            @pl.when(odd)
            def _(e=e, c=c):
                relay(e, c).wait_send()
    for i in range(last + 1):
        for c in range(chunks):
            @pl.when(has_lo)
            def _(i=i, c=c):
                to_lo(i, c).wait_send()

            @pl.when(has_hi)
            def _(i=i, c=c):
                to_hi(i, c).wait_send()
    for c in range(chunks):
        pltpu.make_async_copy(
            V.at[last, pl.ds(1, planes), padded(c)], p_out.at[0, :, rows(c)], out_sem.at[0, c]
        ).wait()
        pltpu.make_async_copy(R.at[:, rows(c)], r_out.at[0, :, rows(c)], out_sem.at[1, c]).wait()


def solution(mesh):
    n_tm, n_space = mesh.shape["tm"], mesh.shape["space"]
    placed = (
        P("tm", "space", None, None),
        P("tm", "space", None, None),
        P("space", None, None),
        P("tm", "space", None, None),
    )

    def body(forcing, inv_density, wall_mask, guess):
        planes, height, width = wall_mask.shape
        chunks = height // ROWS
        full = (planes, height, width)
        exchanges = ITERS + 1
        values = 2 * ITERS + 1
        f32 = jnp.float32
        pressure, residual = pl.pallas_call(
            functools.partial(kernel, n_tm, n_space),
            out_shape=[jax.ShapeDtypeStruct(guess.shape, f32)] * 2,
            in_specs=[pl.BlockSpec(memory_space=pl.ANY)] * 4,
            out_specs=[pl.BlockSpec(memory_space=pl.ANY)] * 2,
            scratch_shapes=[
                pltpu.VMEM((values, planes + 2, height + 2 * PAD, width), f32),
                pltpu.VMEM((exchanges,) + full, f32),
                pltpu.VMEM((exchanges,) + full, f32),
                pltpu.VMEM(full, f32),
                pltpu.VMEM(full, inv_density.dtype),
                pltpu.VMEM(full, wall_mask.dtype),
                pltpu.VMEM(full, f32),
                pltpu.VMEM(full, f32),
                pltpu.VMEM(full, f32),
                pltpu.VMEM(full, f32),
                pltpu.VMEM(full, f32),
                pltpu.VMEM(full, f32),
                pltpu.SemaphoreType.DMA((4,)),
                pltpu.SemaphoreType.DMA((2, chunks)),
                pltpu.SemaphoreType.DMA((exchanges, chunks)),
                pltpu.SemaphoreType.DMA((exchanges, chunks)),
                pltpu.SemaphoreType.DMA((exchanges, chunks)),
                pltpu.SemaphoreType.DMA((exchanges, chunks)),
                pltpu.SemaphoreType.DMA((values, 2, chunks)),
                pltpu.SemaphoreType.DMA((values, 2, chunks)),
            ],
            compiler_params=pltpu.CompilerParams(collective_id=0, has_side_effects=True),
        )(forcing, inv_density, wall_mask, guess)
        return pressure, residual

    return jax.shard_map(
        body,
        mesh=mesh,
        in_specs=placed,
        out_specs=(P("tm", "space", None, None), P("tm", "space", None, None)),
        check_vma=False,
    )
```

time: 96.5 us -> 52.5 us (0.54)
  waiting for transfers between devices: 53.9 us -> 0 us
  Pallas kernels: 0 us -> 49 us
  starting transfers between devices: 34.5 us -> 0 us
  other arithmetic: 5.88 us -> 0 us
  local copies, waits for them, and re-layouts: 1.09 us -> 2.74 us
    ppermute x16 -> x0, waiting for transfers between devices: 53.9 us -> none  [the longest x6 44.3 us: from_behind(): return lax.ppermute(block, axis, route)]
    pallas_call x0 -> x1, Pallas kernels: none -> 49 us  [body(): pl.pallas_call(functools.partial(kernel, n_tm, n_space), out_shape=[jax.S...]
    ppermute x16 -> x0, starting transfers between devices: 34.5 us -> none  [the longest x5 18.4 us: padded_2(): lax.ppermute(tail, axis, [(i, (i + 1) % count) for i in range(ends)])]
    mul x5 -> x0, other arithmetic: 5.88 us -> none  [the longest x4 4.54 us: body(): mask_all * ((source + density_all * beside_all(extend_slab(value))) / sca...]
    unnamed x8 -> x4, local copies, waits for them, and re-layouts: 0.02 us -> 2.74 us
    slice x5 -> x0, local copies, waits for them, and re-layouts: 1.07 us -> none  [padded_2(): head = lax.slice_in_dim(cells, 0, width, axis=dim)]
  transfers between devices with their start and end apart: 16 -> 0, of which waited for: 16 -> 0; matrix products, arithmetic and copies ran while one was open for 1% -> 0% of each run, Pallas kernels for 0% -> 0%
where the time goes in v1:
time: 52.5 us; the launch traced here: 52.3 us
  Pallas kernels  49 us (93%)
  local copies, waits for them, and re-layouts  2.74 us (5%)
  between operations  0.65 us (1%)
    pallas_call x1, Pallas kernels, body(): pl.pallas_call(functools.partial(kernel, n_tm, n_space), out_shape=[jax.S...  49 us
    unnamed x4, local copies, waits for them, and re-layouts  2.74 us

profile of v1, /device:TPU:1, one launch (start us, length us, event | category | flops | bytes accessed | tf_op | source)
XLA Modules:
  0.0 52.3 jit_solution(12724392827136653235)
XLA Ops:
  0.6 49.0 %shard_map.59 = (f32[1,4,32,1024]{3,2,1,0:T(8,128)}, f32[1,4,32,1024]{3,2,1,0:T(8,128)}) custom-call(f32[1,4,32,1024]{3,2,1,0:T(8,128)} %f_hbm.1, bf16[1,4,32,1024]{3,2,1,0:T(8,128)(2,1)} %k_hbm.1, s32[4,32,1024]{2,1,0:T(8,128)} %m_hbm.1, f32[1,4,32,1024]{3,2,1,0:T(8,128)} %g_hbm.1), custom_call_target="tpu_custom_call" | custom-call | tf_op jit(solution)/shard_map/pallas_call | solution.py:284
  49.6 0.0 copy-start
  49.6 1.9 %copy.8 = f32[1,4,32,1024]{3,2,1,0:T(8,128)} copy(f32[1,4,32,1024]{3,2,1,0:T(8,128)} %get-tuple-element.4) | data formatting | bytes 1048576
  51.5 0.0 copy-done
  51.5 0.8 %copy.9 = f32[1,4,32,1024]{3,2,1,0:T(8,128)} copy(f32[1,4,32,1024]{3,2,1,0:T(8,128)S(1)} %copy-done) | data formatting | bytes 1048576
Async XLA Ops:
  49.6 2.0 %copy-start = (f32[1,4,32,1024]{3,2,1,0:T(8,128)S(1)}, f32[1,4,32,1024]{3,2,1,0:T(8,128)}, u32[]{:S(2)}) copy-start(f32[1,4,32,1024]{3,2,1,0:T(8,128)} %get-tuple-element.5) | copy-start | bytes 1572868

commit v2 on v1

--- a/solution.py
+++ b/solution.py
@@ -16,7 +16,7 @@
     n_tm, n_space,
     f_hbm, k_hbm, m_hbm, g_hbm, p_out, r_out,
     V, A, B, F, K, M, W, KW, MD, MK, G, R,
-    load_sem, out_sem, sa, ra, sb, rb, sh, rh,
+    load_sem, sa, ra, sb, rb, sh, rh,
 ):
     planes, height, width = F.shape
     chunks = height // ROWS
@@ -185,7 +185,10 @@
     def sweep_second(e, c):
         def step(p, _):
             at = rows(c)
-            V[2 * e + 2, p + 1, padded(c), :] = G[p, at, :] + KW[p, at, :] * beside(2 * e + 1, p, c)[1]
+            v = G[p, at, :] + KW[p, at, :] * beside(2 * e + 1, p, c)[1]
+            V[2 * e + 2, p + 1, padded(c), :] = v
+            if e == ITERS - 1:
+                p_out[0, p, at, :] = v
             return 0
         lax.fori_loop(0, planes, step, 0)
 
@@ -201,10 +204,6 @@
         sweep_second(e, c)
         send_field(e + 1, c)
         send_halo(2 * e + 2, c)
-        if e == ITERS - 1:
-            pltpu.make_async_copy(
-                V.at[last, pl.ds(1, planes), padded(c)], p_out.at[0, :, rows(c)], out_sem.at[0, c]
-            ).start()
 
     for e in range(ITERS):
         for c in range(chunks):
@@ -233,10 +232,9 @@
         def complete(p, _, c=c):
             at = rows(c)
             m = M[p, at, :].astype(jnp.float32)
-            R[p, at, :] = R[p, at, :] + m * (2.0 * A[ITERS, p, at, :] - 0.5 * B[ITERS, p, at, :])
+            r_out[0, p, at, :] = R[p, at, :] + m * (2.0 * A[ITERS, p, at, :] - 0.5 * B[ITERS, p, at, :])
             return 0
         lax.fori_loop(0, planes, complete, 0)
-        pltpu.make_async_copy(R.at[:, rows(c)], r_out.at[0, :, rows(c)], out_sem.at[1, c]).start()
 
     for e in range(ITERS + 1):
         for c in range(chunks):
@@ -258,11 +256,6 @@
             @pl.when(has_hi)
             def _(i=i, c=c):
                 to_hi(i, c).wait_send()
-    for c in range(chunks):
-        pltpu.make_async_copy(
-            V.at[last, pl.ds(1, planes), padded(c)], p_out.at[0, :, rows(c)], out_sem.at[0, c]
-        ).wait()
-        pltpu.make_async_copy(R.at[:, rows(c)], r_out.at[0, :, rows(c)], out_sem.at[1, c]).wait()
 
 
 def solution(mesh):
@@ -283,9 +276,9 @@
         f32 = jnp.float32
         pressure, residual = pl.pallas_call(
             functools.partial(kernel, n_tm, n_space),
-            out_shape=[jax.ShapeDtypeStruct(guess.shape, f32)] * 2,
+            out_shape=[pltpu.VMEM(guess.shape, f32)] * 2,
             in_specs=[pl.BlockSpec(memory_space=pl.ANY)] * 4,
-            out_specs=[pl.BlockSpec(memory_space=pl.ANY)] * 2,
+            out_specs=[pl.BlockSpec(memory_space=pltpu.VMEM)] * 2,
             scratch_shapes=[
                 pltpu.VMEM((values, planes + 2, height + 2 * PAD, width), f32),
                 pltpu.VMEM((exchanges,) + full, f32),
@@ -300,7 +293,6 @@
                 pltpu.VMEM(full, f32),
                 pltpu.VMEM(full, f32),
                 pltpu.SemaphoreType.DMA((4,)),
-                pltpu.SemaphoreType.DMA((2, chunks)),
                 pltpu.SemaphoreType.DMA((exchanges, chunks)),
                 pltpu.SemaphoreType.DMA((exchanges, chunks)),
                 pltpu.SemaphoreType.DMA((exchanges, chunks)),

time: 52.5 us -> 50.7 us (0.966)
  local copies, waits for them, and re-layouts: 2.74 us -> 1.59 us
  Pallas kernels: 49 us -> 48.3 us
    unnamed x4 -> x2, local copies, waits for them, and re-layouts: 2.74 us -> 1.59 us
    pallas_call x1, Pallas kernels: 49 us -> 48.3 us  [body(): pl.pallas_call(functools.partial(kernel, n_tm, n_space), out_shape=[pltpu...]
where the time goes in v2:
time: 50.7 us; the launch traced here: 50.6 us
  Pallas kernels  48.3 us (95%)
  local copies, waits for them, and re-layouts  1.59 us (3%)
  between operations  0.64 us (1%)
    pallas_call x1, Pallas kernels, body(): pl.pallas_call(functools.partial(kernel, n_tm, n_space), out_shape=[pltpu...  48.3 us
    unnamed x2, local copies, waits for them, and re-layouts  1.59 us

profile of v2, /device:TPU:1, one launch (start us, length us, event | category | flops | bytes accessed | tf_op | source)
XLA Modules:
  0.0 50.6 jit_solution(16718872456067404807)
XLA Ops:
  0.6 48.3 %shard_map.59 = (f32[1,4,32,1024]{3,2,1,0:T(8,128)S(1)}, f32[1,4,32,1024]{3,2,1,0:T(8,128)S(1)}) custom-call(f32[1,4,32,1024]{3,2,1,0:T(8,128)} %f_hbm.1, bf16[1,4,32,1024]{3,2,1,0:T(8,128)(2,1)} %k_hbm.1, s32[4,32,1024]{2,1,0:T(8,128)} %m_hbm.1, f32[1,4,32,1024]{3,2,1,0:T(8,128)} %g_hbm.1), custom_call_target="tpu_custom_call" | custom-call | tf_op jit(solution)/shard_map/pallas_call | solution.py:277
  49.0 0.8 %copy.8 = f32[1,4,32,1024]{3,2,1,0:T(8,128)} copy(f32[1,4,32,1024]{3,2,1,0:T(8,128)S(1)} %get-tuple-element.2) | data formatting | bytes 1048576
  49.8 0.8 %copy.9 = f32[1,4,32,1024]{3,2,1,0:T(8,128)} copy(f32[1,4,32,1024]{3,2,1,0:T(8,128)S(1)} %get-tuple-element.3) | data formatting | bytes 1048576

commit v3 on v2

--- a/solution.py
+++ b/solution.py
@@ -10,6 +10,7 @@
 ITERS = 2
 ROWS = 8
 PAD = 8
+PARTS = 2
 
 
 def kernel(
@@ -46,7 +47,7 @@
         load.start()
 
     barrier = pltpu.get_barrier_semaphore()
-    for other in (partner, ahead, behind):
+    for other in (partner, behind):
         pl.semaphore_signal(barrier, inc=1, device_id={"tm": other}, device_id_type=pl.DeviceIdType.MESH)
 
     @pl.when(has_lo)
@@ -59,30 +60,35 @@
 
     @pl.when(has_lo & has_hi)
     def _():
-        pl.semaphore_wait(barrier, 5)
+        pl.semaphore_wait(barrier, 4)
 
     @pl.when(jnp.logical_not(has_lo & has_hi))
     def _():
-        pl.semaphore_wait(barrier, 4)
-
-    def field(e, c):
+        pl.semaphore_wait(barrier, 3)
+
+    share = planes // PARTS
+
+    def part(q):
+        return pl.ds(q * share, share)
+
+    def field(e, c, q):
         if e == 0:
-            return g_hbm.at[0, :, rows(c)]
-        return V.at[2 * e, pl.ds(1, planes), padded(c)]
-
-    def to_ahead(e, c):
-        return pltpu.make_async_remote_copy(
-            field(e, c), B.at[e, :, rows(c)], sb.at[e, c], rb.at[e, c],
+            return g_hbm.at[0, part(q), rows(c)]
+        return V.at[2 * e, pl.ds(1 + q * share, share), padded(c)]
+
+    def to_ahead(e, c, q):
+        return pltpu.make_async_remote_copy(
+            field(e, c, q), B.at[e, part(q), rows(c)], sb.at[e, c, q], rb.at[e, c, q],
             device_id={"tm": ahead}, device_id_type=pl.DeviceIdType.MESH)
 
-    def to_partner(e, c):
-        return pltpu.make_async_remote_copy(
-            field(e, c), A.at[e, :, rows(c)], sa.at[e, c], ra.at[e, c],
+    def to_partner(e, c, q):
+        return pltpu.make_async_remote_copy(
+            field(e, c, q), A.at[e, part(q), rows(c)], sa.at[e, c, q], ra.at[e, c, q],
             device_id={"tm": partner}, device_id_type=pl.DeviceIdType.MESH)
 
-    def relay(e, c):
-        return pltpu.make_async_remote_copy(
-            B.at[e, :, rows(c)], A.at[e, :, rows(c)], sa.at[e, c], ra.at[e, c],
+    def relay(e, c, q):
+        return pltpu.make_async_remote_copy(
+            B.at[e, part(q), rows(c)], A.at[e, part(q), rows(c)], sa.at[e, c, q], ra.at[e, c, q],
             device_id={"tm": partner}, device_id_type=pl.DeviceIdType.MESH)
 
     def to_lo(i, c):
@@ -98,11 +104,13 @@
             device_id={"space": s + 1}, device_id_type=pl.DeviceIdType.MESH)
 
     def send_field(e, c):
-        to_ahead(e, c).start()
+        for q in range(PARTS):
+            to_ahead(e, c, q).start()
 
         @pl.when(even)
         def _():
-            to_partner(e, c).start()
+            for q in range(PARTS):
+                to_partner(e, c, q).start()
 
     def send_halo(i, c):
         @pl.when(has_lo)
@@ -193,11 +201,16 @@
         lax.fori_loop(0, planes, step, 0)
 
     def arrive(e, c):
-        to_ahead(e, c).wait_recv()
-
-        @pl.when(odd)
-        def _():
-            relay(e, c).start()
+        for q in range(PARTS):
+            to_ahead(e, c, q).wait_recv()
+
+            @pl.when(odd)
+            def _(q=q):
+                relay(e, c, q).start()
+
+    def arrive_last(e, c):
+        for q in range(PARTS):
+            to_partner(e, c, q).wait_recv()
 
     def finish(e, c):
         wait_halo(2 * e + 1, c)
@@ -209,7 +222,7 @@
         for c in range(chunks):
             arrive(e, c)
             wait_halo(2 * e, c)
-            to_partner(e, c).wait_recv()
+            arrive_last(e, c)
             sweep_first(e, c)
             send_halo(2 * e + 1, c)
             if c >= 1:
@@ -227,7 +240,7 @@
             R[p, at, :] = m * F[p, at, :] - MD[p, at, :] * mid + MK[p, at, :] * total
             return 0
         lax.fori_loop(0, planes, partial, 0)
-        to_partner(ITERS, c).wait_recv()
+        arrive_last(ITERS, c)
 
         def complete(p, _, c=c):
             at = rows(c)
@@ -238,15 +251,18 @@
 
     for e in range(ITERS + 1):
         for c in range(chunks):
-            to_ahead(e, c).wait_send()
+            for q in range(PARTS):
+                to_ahead(e, c, q).wait_send()
 
             @pl.when(even)
             def _(e=e, c=c):
-                to_partner(e, c).wait_send()
+                for q in range(PARTS):
+                    to_partner(e, c, q).wait_send()
 
             @pl.when(odd)
             def _(e=e, c=c):
-                relay(e, c).wait_send()
+                for q in range(PARTS):
+                    relay(e, c, q).wait_send()
     for i in range(last + 1):
         for c in range(chunks):
             @pl.when(has_lo)
@@ -293,10 +309,10 @@
                 pltpu.VMEM(full, f32),
                 pltpu.VMEM(full, f32),
                 pltpu.SemaphoreType.DMA((4,)),
-                pltpu.SemaphoreType.DMA((exchanges, chunks)),
-                pltpu.SemaphoreType.DMA((exchanges, chunks)),
-                pltpu.SemaphoreType.DMA((exchanges, chunks)),
-                pltpu.SemaphoreType.DMA((exchanges, chunks)),
+                pltpu.SemaphoreType.DMA((exchanges, chunks, PARTS)),
+                pltpu.SemaphoreType.DMA((exchanges, chunks, PARTS)),
+                pltpu.SemaphoreType.DMA((exchanges, chunks, PARTS)),
+                pltpu.SemaphoreType.DMA((exchanges, chunks, PARTS)),
                 pltpu.SemaphoreType.DMA((values, 2, chunks)),
                 pltpu.SemaphoreType.DMA((values, 2, chunks)),
             ],

time: 50.7 us -> 50.1 us (0.988)
  Pallas kernels: 48.3 us -> 47.7 us
    pallas_call x1, Pallas kernels: 48.3 us -> 47.7 us  [body(): pl.pallas_call(functools.partial(kernel, n_tm, n_space), out_shape=[pltpu...]
where the time goes in v3:
time: 50.1 us; the launch traced here: 49.9 us
  Pallas kernels  47.7 us (95%)
  local copies, waits for them, and re-layouts  1.59 us (3%)
  between operations  0.64 us (1%)
    pallas_call x1, Pallas kernels, body(): pl.pallas_call(functools.partial(kernel, n_tm, n_space), out_shape=[pltpu...  47.7 us
    unnamed x2, local copies, waits for them, and re-layouts  1.59 us

profile of v3, /device:TPU:1, one launch (start us, length us, event | category | flops | bytes accessed | tf_op | source)
XLA Modules:
  0.0 49.9 jit_solution(11256892993410466767)
XLA Ops:
  0.6 47.7 %shard_map.59 = (f32[1,4,32,1024]{3,2,1,0:T(8,128)S(1)}, f32[1,4,32,1024]{3,2,1,0:T(8,128)S(1)}) custom-call(f32[1,4,32,1024]{3,2,1,0:T(8,128)} %f_hbm.1, bf16[1,4,32,1024]{3,2,1,0:T(8,128)(2,1)} %k_hbm.1, s32[4,32,1024]{2,1,0:T(8,128)} %m_hbm.1, f32[1,4,32,1024]{3,2,1,0:T(8,128)} %g_hbm.1), custom_call_target="tpu_custom_call" | custom-call | tf_op jit(solution)/shard_map/pallas_call | solution.py:293
  48.4 0.8 %copy.8 = f32[1,4,32,1024]{3,2,1,0:T(8,128)} copy(f32[1,4,32,1024]{3,2,1,0:T(8,128)S(1)} %get-tuple-element.2) | data formatting | bytes 1048576
  49.1 0.8 %copy.9 = f32[1,4,32,1024]{3,2,1,0:T(8,128)} copy(f32[1,4,32,1024]{3,2,1,0:T(8,128)S(1)} %get-tuple-element.3) | data formatting | bytes 1048576

commit v4 on v3

--- a/solution.py
+++ b/solution.py
@@ -10,7 +10,7 @@
 ITERS = 2
 ROWS = 8
 PAD = 8
-PARTS = 2
+PARTS = 4
 
 
 def kernel(
@@ -274,6 +274,18 @@
                 to_hi(i, c).wait_send()
 
 
+def write_out(p_ref, r_ref, p_out, r_out, sem):
+    planes = p_ref.shape[1]
+    copies = []
+    for i, (src, dst) in enumerate(((p_ref, p_out), (r_ref, r_out))):
+        for p in range(planes):
+            copies.append(pltpu.make_async_copy(src.at[0, p], dst.at[0, p], sem.at[i, p]))
+    for copy in copies:
+        copy.start()
+    for copy in copies:
+        copy.wait()
+
+
 def solution(mesh):
     n_tm, n_space = mesh.shape["tm"], mesh.shape["space"]
     placed = (
@@ -318,7 +330,13 @@
             ],
             compiler_params=pltpu.CompilerParams(collective_id=0, has_side_effects=True),
         )(forcing, inv_density, wall_mask, guess)
-        return pressure, residual
+        return pl.pallas_call(
+            write_out,
+            out_shape=(jax.ShapeDtypeStruct(guess.shape, f32),) * 2,
+            in_specs=[pl.BlockSpec(memory_space=pltpu.VMEM)] * 2,
+            out_specs=(pl.BlockSpec(memory_space=pl.ANY),) * 2,
+            scratch_shapes=[pltpu.SemaphoreType.DMA((2, planes))],
+        )(*[pltpu.with_memory_space_constraint(v, pltpu.VMEM) for v in (pressure, residual)])
 
     return jax.shard_map(
         body,

time: 50.1 us -> 50.1 us (level)
  Pallas kernels: 47.7 us -> 49.3 us
  local copies, waits for them, and re-layouts: 1.59 us -> 0 us
    unnamed x2 -> x0, local copies, waits for them, and re-layouts: 1.59 us -> none
    pallas_call x0 -> x1, Pallas kernels: none -> 1.03 us  [body(): pl.pallas_call(write_out, out_shape=(jax.ShapeDtypeStruct(guess.shape, f3...]
    pallas_call x1, Pallas kernels: 47.7 us -> 48.3 us  [body(): pl.pallas_call(functools.partial(kernel, n_tm, n_space), out_shape=[pltpu...]
where the time goes in v4:
time: 50.1 us; the launch traced here: 49.9 us
  Pallas kernels  49.3 us (98%)
  between operations  0.64 us (1%)
    pallas_call x1, Pallas kernels, body(): pl.pallas_call(functools.partial(kernel, n_tm, n_space), out_shape=[pltpu...  48.3 us
    pallas_call x1, Pallas kernels, body(): pl.pallas_call(write_out, out_shape=(jax.ShapeDtypeStruct(guess.shape, f3...  1.03 us

profile of v4, /device:TPU:1, one launch (start us, length us, event | category | flops | bytes accessed | tf_op | source)
XLA Modules:
  0.0 49.9 jit_solution(9665629347884692449)
XLA Ops:
  0.6 48.3 %shard_map.59 = (f32[1,4,32,1024]{3,2,1,0:T(8,128)S(1)}, f32[1,4,32,1024]{3,2,1,0:T(8,128)S(1)}) custom-call(f32[1,4,32,1024]{3,2,1,0:T(8,128)} %f_hbm.1, bf16[1,4,32,1024]{3,2,1,0:T(8,128)(2,1)} %k_hbm.1, s32[4,32,1024]{2,1,0:T(8,128)} %m_hbm.1, f32[1,4,32,1024]{3,2,1,0:T(8,128)} %g_hbm.1), custom_call_target="tpu_custom_call" | custom-call | tf_op jit(solution)/shard_map/pallas_call | solution.py:305
  48.9 1.0 %shard_map.60 = (f32[1,4,32,1024]{3,2,1,0:T(8,128)}, f32[1,4,32,1024]{3,2,1,0:T(8,128)}) custom-call(f32[1,4,32,1024]{3,2,1,0:T(8,128)S(1)} %get-tuple-element.4.p_ref, f32[1,4,32,1024]{3,2,1,0:T(8,128)S(1)} %get-tuple-element.5.r_ref), custom_call_target="tpu_custom_call" | custom-call | tf_op jit(solution)/shard_map/pallas_call | solution.py:333

commit v5 on v4

--- a/solution.py
+++ b/solution.py
@@ -10,7 +10,7 @@
 ITERS = 2
 ROWS = 8
 PAD = 8
-PARTS = 4
+PARTS = 2
 
 
 def kernel(

time: 50.1 us -> 49.5 us (0.988)
  Pallas kernels: 49.3 us -> 48.7 us
    pallas_call x1, Pallas kernels: 48.3 us -> 47.7 us  [body(): pl.pallas_call(functools.partial(kernel, n_tm, n_space), out_shape=[pltpu...]
where the time goes in v5:
time: 49.5 us; the launch traced here: 49.4 us
  Pallas kernels  48.7 us (98%)
  between operations  0.64 us (1%)
    pallas_call x1, Pallas kernels, body(): pl.pallas_call(functools.partial(kernel, n_tm, n_space), out_shape=[pltpu...  47.7 us
    pallas_call x1, Pallas kernels, body(): pl.pallas_call(write_out, out_shape=(jax.ShapeDtypeStruct(guess.shape, f3...  1.03 us

profile of v5, /device:TPU:1, one launch (start us, length us, event | category | flops | bytes accessed | tf_op | source)
XLA Modules:
  0.0 49.4 jit_solution(12033493666176556506)
XLA Ops:
  0.6 47.7 %shard_map.59 = (f32[1,4,32,1024]{3,2,1,0:T(8,128)S(1)}, f32[1,4,32,1024]{3,2,1,0:T(8,128)S(1)}) custom-call(f32[1,4,32,1024]{3,2,1,0:T(8,128)} %f_hbm.1, bf16[1,4,32,1024]{3,2,1,0:T(8,128)(2,1)} %k_hbm.1, s32[4,32,1024]{2,1,0:T(8,128)} %m_hbm.1, f32[1,4,32,1024]{3,2,1,0:T(8,128)} %g_hbm.1), custom_call_target="tpu_custom_call" | custom-call | tf_op jit(solution)/shard_map/pallas_call | solution.py:305
  48.4 1.0 %shard_map.60 = (f32[1,4,32,1024]{3,2,1,0:T(8,128)}, f32[1,4,32,1024]{3,2,1,0:T(8,128)}) custom-call(f32[1,4,32,1024]{3,2,1,0:T(8,128)S(1)} %get-tuple-element.4.p_ref, f32[1,4,32,1024]{3,2,1,0:T(8,128)S(1)} %get-tuple-element.5.r_ref), custom_call_target="tpu_custom_call" | custom-call | tf_op jit(solution)/shard_map/pallas_call | solution.py:333

commit v6 on v5

--- a/solution.py
+++ b/solution.py
@@ -43,9 +43,6 @@
         pltpu.make_async_copy(m_hbm, M, load_sem.at[2]),
         pltpu.make_async_copy(f_hbm.at[0], F, load_sem.at[3]),
     ]
-    for load in loads:
-        load.start()
-
     barrier = pltpu.get_barrier_semaphore()
     for other in (partner, behind):
         pl.semaphore_signal(barrier, inc=1, device_id={"tm": other}, device_id_type=pl.DeviceIdType.MESH)
@@ -57,6 +54,9 @@
     @pl.when(has_hi)
     def _():
         pl.semaphore_signal(barrier, inc=1, device_id={"space": s + 1}, device_id_type=pl.DeviceIdType.MESH)
+
+    for load in loads:
+        load.start()
 
     @pl.when(has_lo & has_hi)
     def _():

time: 49.5 us -> 49.5 us (level)
  no operation moved by 1% of the time
where the time goes in v6:
time: 49.5 us; the launch traced here: 49.4 us
  Pallas kernels  48.7 us (98%)
  between operations  0.64 us (1%)
    pallas_call x1, Pallas kernels, body(): pl.pallas_call(functools.partial(kernel, n_tm, n_space), out_shape=[pltpu...  47.7 us
    pallas_call x1, Pallas kernels, body(): pl.pallas_call(write_out, out_shape=(jax.ShapeDtypeStruct(guess.shape, f3...  1.03 us

profile of v6, /device:TPU:1, one launch (start us, length us, event | category | flops | bytes accessed | tf_op | source)
XLA Modules:
  0.0 49.4 jit_solution(849199700202329629)
XLA Ops:
  0.6 47.7 %shard_map.59 = (f32[1,4,32,1024]{3,2,1,0:T(8,128)S(1)}, f32[1,4,32,1024]{3,2,1,0:T(8,128)S(1)}) custom-call(f32[1,4,32,1024]{3,2,1,0:T(8,128)} %f_hbm.1, bf16[1,4,32,1024]{3,2,1,0:T(8,128)(2,1)} %k_hbm.1, s32[4,32,1024]{2,1,0:T(8,128)} %m_hbm.1, f32[1,4,32,1024]{3,2,1,0:T(8,128)} %g_hbm.1), custom_call_target="tpu_custom_call" | custom-call | tf_op jit(solution)/shard_map/pallas_call | solution.py:305
  48.4 1.0 %shard_map.60 = (f32[1,4,32,1024]{3,2,1,0:T(8,128)}, f32[1,4,32,1024]{3,2,1,0:T(8,128)}) custom-call(f32[1,4,32,1024]{3,2,1,0:T(8,128)S(1)} %get-tuple-element.4.p_ref, f32[1,4,32,1024]{3,2,1,0:T(8,128)S(1)} %get-tuple-element.5.r_ref), custom_call_target="tpu_custom_call" | custom-call | tf_op jit(solution)/shard_map/pallas_call | solution.py:333
